TPU v7x, 256 devices: a whole 4x4x8 slice. The times are simulated.
256 devices in a mesh: prompt: 8 (over x, y_lo), tensor: 32 (over z, y_hi, core).
Axes of the slice: x: 4, y: 4 (y_hi: 2, y_lo: 2; y = y_hi * 2 + y_lo), z: 8, core: 2. Of those that a mesh axis runs over, the one named last changes fastest.
Arguments:
- tokens: bfloat16 [8, 128, 8192], P('prompt')
- gate_weight: bfloat16 [8192, 28672], P('prompt', 'tensor'), may hold values from -0.0625 to 0.0625
- up_weight: bfloat16 [8192, 28672], P('prompt', 'tensor'), may hold values from -0.0625 to 0.0625
- down_weight: bfloat16 [28672, 8192], P('tensor', 'prompt')
- norm_gain: float32 [8192], P('prompt'), may hold values from 0.1 to 1.9
- unembed: bfloat16 [8192, 86016], P('prompt', 'tensor'), may hold values from -0.5 to 0.5
- guidance: float32 [8], replicated, may hold values from -1.5 to 2.5
- logit_bias: float32 [128, 86016], P('prompt', 'tensor'), may hold values from -2 to 322
Outputs:
- log_probs: float32 [128, 86016], P('prompt', 'tensor')
All inputs are finite; a program needn't handle non-finite values.
Results may differ from a plain program's by a relative error of at most 0.0025.
Values may be sent and summed in bfloat16 or wider, within the bound.
No kernel may reach another device: no remote copies, remote signals or barrier semaphores. Data moves between devices by JAX's collectives and lax.ppermute only.
A program may use at most 64 MiB of HBM per device.

v0:
```python
import jax
import jax.numpy as jnp
from jax import lax
from jax.sharding import Mesh
from jax.sharding import PartitionSpec as P

D = 8192
PROMPT = ("prompt_0", "prompt_1")


def own_rows(so_far, axes):
    for axis in axes:
        so_far = lax.psum_scatter(so_far, axis, scatter_dimension=0, tiled=True)
    return so_far


def copy_for_each(array, axis):
    peers = lax.axis_size(axis)
    return lax.all_to_all(
        jnp.broadcast_to(array[None], (peers, *array.shape)), axis, 0, 0, tiled=True
    )


def joined_along(tiles, dim):
    tiles = jnp.moveaxis(tiles, 0, dim)
    shape = tiles.shape
    return tiles.reshape(*shape[:dim], shape[dim] * shape[dim + 1], *shape[dim + 2 :])


def collect(array, axis, dim):
    tiles = copy_for_each(array, axis)
    return joined_along(tiles, dim)


def of_everyone(array, axis):
    return copy_for_each(array, axis).sum(axis=0)


def cut_along(array, dim, peers):
    shape = array.shape
    tiles = array.reshape(*shape[:dim], peers, shape[dim] // peers, *shape[dim + 1 :])
    return jnp.moveaxis(tiles, dim, 0)


def sent_and_summed(array, axis, dim):
    tiles = cut_along(array, dim, lax.axis_size(axis))
    arrived = lax.all_to_all(tiles, axis, split_axis=0, concat_axis=0, tiled=True)
    return arrived.sum(axis=0)


def gathered_once(array, axis):
    leaves = jax.tree.leaves(array)
    turns = sorted(range(len(leaves)), key=lambda k: -leaves[k].size)
    width = (1, *leaves[turns[0]].shape)[-1]
    lines = [
        jnp.pad(leaves[k].reshape(-1), (0, -leaves[k].size % width)).reshape(-1, width)
        for k in turns
    ]
    both, at, found = (copy_for_each(jnp.concatenate(lines), axis), 0, {})
    for k, line in zip(turns, lines):
        slab = both[:, at : at + len(line)].reshape(len(both), -1)
        found[k] = slab[:, : leaves[k].size].reshape(-1, *leaves[k].shape)
        at += len(line)
    numbers = iter(range(len(leaves)))
    return jax.tree.map(lambda _: found[next(numbers)], array)


def combined_pairwise(pieces, combine):
    while len(jax.tree.leaves(pieces)[0]) > 1:
        pieces = jax.vmap(combine)(
            *(jax.tree.map(lambda part: part[side::2], pieces) for side in (0, 1))
        )
    return jax.tree.map(lambda part: part[0], pieces)


def merged(array, axis, combine):
    pieces = gathered_once(array, axis)
    return combined_pairwise(pieces, combine)


def combine_lse(first, second):
    top = jnp.maximum(first[0], second[0])
    total = first[1] * jnp.exp(first[0] - top) + second[1] * jnp.exp(second[0] - top)
    return (top, total)


def local(tokens, gate_weight, up_weight, down_weight, norm_gain, unembed, guidance, logit_bias):
    variants = lax.axis_size(PROMPT)
    rows = tokens.shape[1]
    share = gate_weight.shape[0]
    spread = lax.all_to_all(tokens, PROMPT, split_axis=2, concat_axis=0, tiled=True)
    flat = spread.reshape(variants * rows, share)
    gate_part = jnp.dot(flat, gate_weight, preferred_element_type=jnp.float32)
    up_part = jnp.dot(flat, up_weight, preferred_element_type=jnp.float32)
    gate_up = own_rows(jnp.concatenate([gate_part, up_part], axis=1), PROMPT)
    width = gate_weight.shape[1]
    hidden = (jax.nn.silu(gate_up[:, :width]) * gate_up[:, width:]).astype(jnp.bfloat16)
    partial_branch = jnp.dot(
        collect(hidden, PROMPT, 0), down_weight, preferred_element_type=jnp.float32
    )
    mine = lax.psum_scatter(partial_branch, "tensor", scatter_dimension=0, tiled=True)
    count = mine.shape[0]
    start = lax.axis_index("tensor") * count
    state = lax.dynamic_slice_in_dim(flat, start, count, 0).astype(jnp.float32) + mine
    square = of_everyone(jnp.sum(state * state, axis=1), PROMPT)
    owned = (state * lax.rsqrt(square / D + 1e-05)[:, None] * norm_gain).astype(jnp.bfloat16)
    normed = lax.all_gather(owned, "tensor", axis=0, tiled=True)
    blocks = normed.reshape(variants, rows, share)
    mixed = jnp.tensordot(guidance, blocks.astype(jnp.float32), axes=1)
    high = mixed.astype(jnp.bfloat16)
    low = (mixed - high.astype(jnp.float32)).astype(jnp.bfloat16)
    stacked = jnp.concatenate([high, low], axis=0)
    product = jnp.dot(stacked, unembed, preferred_element_type=jnp.float32)
    scores = (
        sent_and_summed(
            product[: rows // variants * lax.axis_size(PROMPT)]
            + product[rows // variants * lax.axis_size(PROMPT) :],
            PROMPT,
            0,
        )
        + logit_bias
    )
    local_top = jnp.max(scores, axis=1)
    local_total = jnp.sum(jnp.exp(scores - local_top[:, None]), axis=1)
    top, total_exp = merged((local_top, local_total), "tensor", combine_lse)
    return scores - top[:, None] - jnp.log(total_exp)[:, None]


def solution(mesh):
    finer = Mesh(
        mesh.devices.reshape(4, 2, mesh.shape["tensor"]), ("prompt_0", "prompt_1", "tensor")
    )
    placed = (
        P(PROMPT, None, None),
        P(PROMPT, "tensor"),
        P(PROMPT, "tensor"),
        P("tensor", PROMPT),
        P(PROMPT),
        P(PROMPT, "tensor"),
        P(),
        P(PROMPT, "tensor"),
    )
    return jax.shard_map(
        local, mesh=finer, in_specs=placed, out_specs=P(PROMPT, "tensor"), check_vma=False
    )
```

profile of v0, /device:TPU:1, one launch (start us, length us, event | category | flops | bytes accessed | tf_op | source)
XLA Modules:
  0.0 547.3 jit_solution(13178497889290529071)
XLA Ops:
  6.5 0.0 copy-start
  6.5 0.0 reduce-scatter.4.cloned.1.call-start
  6.5 9.6 %copy.23 = bf16[1,128,8192]{1,0,2:T(2,128)(2,1)} copy(bf16[1,128,8192]{2,1,0:T(8,128)(2,1)} %param.8) | data formatting | bytes 4194304 | tf_op args[0]
  16.2 0.5 broadcast.18
  16.7 46.5 %reduce.1 = bf16[8192,128]{1,0:T(8,128)(2,1)} reduce(bf16[8192,1,128]{2,1,0:T(2,128)(2,1)} %bitcast.47, bf16[]{:T(256)} %broadcast.18), dimensions={1}, to_apply=%bitcast.29.reduce_sub_computation | reduce | bytes 4194306
  63.2 5.8 %reshape.57 = bf16[8,2,65536]{2,1,0:T(2,128)(2,1)} reshape(bf16[8192,128]{1,0:T(8,128)(2,1)} %reduce.1) | data formatting | bytes 4194304
  69.0 31.1 %all_to_all.36 = bf16[8,2,65536]{2,1,0:T(2,128)(2,1)} all-to-all(bf16[8,2,65536]{2,1,0:T(2,128)(2,1)} %reshape.57), channel_id=1, replica_groups=mesh['prompt_0'=4,'prompt_1'=2,'tensor'=32] {'prompt_0','prompt_1'}, dimensions={0} | all-to-all | bytes 4194304 | tf_op jit(solution)/shard_map/all_to_all | solution.py:91
  100.1 6.8 %reshape.58 = bf16[8192,1,128]{2,1,0:T(2,128)(2,1)} reshape(bf16[8,2,65536]{2,1,0:T(2,128)(2,1)} %all_to_all.36) | data formatting | bytes 4194304
  106.8 3.8 copy.30
  110.6 4.0 copy.24
  114.6 0.0 copy-start.1
  114.6 0.0 copy-start.5
  114.6 4.5 fusion.15
  119.1 0.0 copy-done.1
  119.1 0.0 copy-done.5
  119.1 2.2 fusion.16
  121.3 3.7 pad_maximum_fusion
  125.0 0.0 reduce-scatter.4.cloned.1.call-update
  125.0 0.0 reduce-scatter.6.cloned.1.call-start
  125.0 78.3 %reduce-scatter.4.cloned.1.call-done = f32[256,1792]{0,1:T(8,128)} async-done(((f32[1024,1792]{0,1:T(8,128)}), f32[256,1792]{0,1:T(8,128)}) %reduce-scatter.4.cloned.1.call-update) | async-done | bytes 1835024 | tf_op jit(solution)/shard_map/reduce_scatter | solution.py:13
  203.3 0.0 reduce-scatter.6.cloned.1.call-update
  203.4 0.2 reduce-scatter.8.cloned.1.call-start
  203.6 36.1 %reduce-scatter.6.cloned.1.call-done = f32[128,1792]{0,1:T(8,128)} async-done(((f32[256,1792]{0,1:T(8,128)}), f32[128,1792]{0,1:T(8,128)}) %reduce-scatter.6.cloned.1.call-update) | async-done | bytes 917520 | tf_op jit(solution)/shard_map/reduce_scatter | solution.py:13
  239.7 1.3 fusion.7
  240.9 0.2 copy.25
  241.1 0.2 broadcast_in_dim.6
  241.4 26.5 %all_to_all.37 = bf16[8,128,896]{2,1,0:T(8,128)(2,1)S(1)} all-to-all(bf16[8,128,896]{2,1,0:T(8,128)(2,1)S(1)} %broadcast_in_dim.6), channel_id=1, replica_groups=mesh['prompt_0'=4,'prompt_1'=2,'tensor'=32] {'prompt_0','prompt_1'}, dimensions={0} | all-to-all | bytes 3670016 | tf_op jit(solution)/shard_map/all_to_all | solution.py:19
  267.9 0.0 copy-done
  267.9 4.3 fusion.17
  272.2 0.0 copy-start.3
  272.2 0.0 copy-start.4
  272.2 0.0 reduce-scatter.8.cloned.1.call-update
  272.2 0.0 all-gather.2.cloned.1.call-start
  272.3 124.4 %reduce-scatter.8.cloned.1.call-done = f32[32,1024]{1,0:T(8,128)} async-done(((f32[1024,1024]{1,0:T(8,128)}), f32[32,1024]{1,0:T(8,128)}) %reduce-scatter.8.cloned.1.call-update) | async-done | bytes 131088 | tf_op jit(solution)/shard_map/reduce_scatter | solution.py:101
  396.6 1.0 multiply_reduce_fusion
  397.7 9.7 %all_to_all.38 = f32[8,1,32]{2,1,0:T(1,128)S(1)} all-to-all(f32[8,1,32]{2,1,0:T(1,128)S(1)} %broadcast_in_dim.7), channel_id=1, replica_groups=mesh['prompt_0'=4,'prompt_1'=2,'tensor'=32] {'prompt_0','prompt_1'}, dimensions={0} | all-to-all | bytes 2048 | tf_op jit(solution)/shard_map/all_to_all | solution.py:19
  407.4 0.0 copy-done.3
  407.4 1.6 multiply_convert_fusion
  409.0 0.0 all-gather.2.cloned.1.call-update
  409.0 83.2 %all-gather.2.cloned.1.call-done = bf16[1024,1024]{1,0:T(8,128)(2,1)} async-done(((bf16[32,1024]{1,0:T(8,128)(2,1)}), bf16[1024,1024]{1,0:T(8,128)(2,1)}) %all-gather.2.cloned.1.call-update) | async-done | bytes 2097168 | tf_op jit(solution)/shard_map/all_gather | solution.py:107
  492.3 0.0 copy-done.4
  492.3 3.0 fusion
  495.3 0.1 copy.38
  495.4 0.1 fusion.6
  495.5 4.2 fusion.2
  499.7 0.1 slice_add_fusion
  499.8 0.0 copy-start.2
  499.9 22.2 %all_to_all.39 = f32[8,16,2688]{2,1,0:T(8,128)S(1)} all-to-all(f32[8,16,2688]{2,1,0:T(8,128)S(1)} %bitcast.50), channel_id=1, replica_groups=mesh['prompt_0'=4,'prompt_1'=2,'tensor'=32] {'prompt_0','prompt_1'}, dimensions={0} | all-to-all | bytes 2752512 | tf_op jit(solution)/shard_map/all_to_all | solution.py:47
  522.0 0.1 reduce_sum.38
  522.1 0.0 copy-done.2
  522.1 0.1 fusion.11
  522.3 0.2 exponential_reduce_fusion
  522.5 17.0 %all_to_all.40 = f32[32,2,16]{2,1,0:T(2,128)S(1)} all-to-all(f32[32,2,16]{2,1,0:T(2,128)S(1)} %broadcast_in_dim.8), channel_id=1, replica_groups=mesh['prompt_0'=4,'prompt_1'=2,'tensor'=32] {'tensor'}, dimensions={0} | all-to-all | bytes 8192 | tf_op jit(solution)/shard_map/all_to_all | solution.py:19
  540.0 0.8 subtract_subtract_fusion
  (27 shorter events, 0.5 us)
Async XLA Ops:
  6.5 261.4 %copy-start = (bf16[896,1024]{1,0:T(8,128)(2,1)S(1)}, bf16[896,1024]{1,0:T(8,128)(2,1)}, u32[]{:S(2)}) copy-start(bf16[896,1024]{1,0:T(8,128)(2,1)} %param.11) | copy-start | bytes 5505028
  6.5 196.8 %reduce-scatter.4.cloned.1.call-start = ((), (), s32[]{:S(2)}) async-start(), calls=%async_computation.8 | async-start | bytes 9175040 | tf_op jit(solution)/shard_map/reduce_scatter | solution.py:13
  114.6 4.5 copy-start.1
  114.6 4.5 copy-start.5
  125.0 114.7 %reduce-scatter.6.cloned.1.call-start = ((), (), s32[]{:S(2)}) async-start(), calls=%async_computation.9 | async-start | bytes 2752512 | tf_op jit(solution)/shard_map/reduce_scatter | solution.py:13
  203.4 193.3 %reduce-scatter.8.cloned.1.call-start = ((), (), s32[]{:S(2)}) async-start(), calls=%async_computation.10 | async-start | bytes 4325376 | tf_op jit(solution)/shard_map/reduce_scatter | solution.py:101
  272.2 135.2 %copy-start.3 = (f32[1024]{0:T(1024)S(1)}, f32[1024]{0:T(1024)}, u32[]{:S(2)}) copy-start(f32[1024]{0:T(1024)} %param.12) | copy-start | bytes 12292
  272.2 220.1 %copy-start.4 = (f32[8]{0:T(128)S(1)}, f32[8]{0:T(128)}, u32[]{:S(2)}) copy-start(f32[8]{0:T(128)} %param.14) | copy-start | bytes 100
  272.2 220.1 %all-gather.2.cloned.1.call-start = ((), (), s32[]{:S(2)}) async-start(), calls=%async_computation.11 | async-start | bytes 2162688 | tf_op jit(solution)/shard_map/all_gather | solution.py:107
  499.8 22.3 %copy-start.2 = (f32[16,2688]{1,0:T(8,128)S(1)}, f32[16,2688]{1,0:T(8,128)}, u32[]{:S(2)}) copy-start(f32[16,2688]{1,0:T(8,128)} %param.15) | copy-start | bytes 516100
Sparse Core Ops, SparseCore 0:
  125.1 78.1 reduce-scatter.3
  205.8 33.7 reduce-scatter.5
  272.3 124.2 reduce-scatter.7
  409.1 83.0 all-gather.1
where the time goes:
time: 548 us; the launch traced here: 547 us
  waiting for transfers between devices  322 us (59%)
  blocking collectives  106 us (19%)
  other arithmetic  55.7 us (10%)
  local copies, waits for them, and re-layouts  31.3 us (6%)
  matrix products  18.1 us (3%)
  between operations  13.3 us (2%)
    reduce_scatter x1, waiting for transfers between devices, local(): lax.psum_scatter(partial_branch, 'tensor', scatter_dimension=0, tiled=True)  124 us
    reduce_scatter x2, waiting for transfers between devices, own_rows(): so_far = lax.psum_scatter(so_far, axis, scatter_dimension=0, tiled=True)  114 us
    all_gather x1, waiting for transfers between devices, local(): normed = lax.all_gather(owned, 'tensor', axis=0, tiled=True)  83.2 us
    all_to_all x3, blocking collectives, copy_for_each(): lax.all_to_all(jnp.broadcast_to(array[None], (peers, *array.shape)), axis...  53.2 us
    unnamed x1, other arithmetic  46.5 us
    all_to_all x1, blocking collectives, local(): lax.all_to_all(tokens, PROMPT, split_axis=2, concat_axis=0, tiled=True)  31.1 us
    unnamed x17, local copies, waits for them, and re-layouts  26.5 us
    all_to_all x1, blocking collectives, sent_and_summed(): lax.all_to_all(tiles, axis, split_axis=0, concat_axis=0, tiled=True)  22.2 us
  transfers between devices with their start and end apart: 4, of which 4 were waited for; matrix products, arithmetic and copies ran while one was open for 0% of the time, Pallas kernels for 0%

commit v1 on v0

--- a/solution.py
+++ b/solution.py
@@ -1,3 +1,4 @@
+import functools
 import jax
 import jax.numpy as jnp
 from jax import lax
@@ -6,6 +7,22 @@
 
 D = 8192
 PROMPT = ("prompt_0", "prompt_1")
+
+
+def assign_terms(page, comm_axis, ndim_at):
+    tmp = jnp.concatenate(
+        lax.all_to_all(
+            jnp.stack(lax.axis_size(comm_axis) * [page]),
+            axis_name=comm_axis,
+            split_axis=0,
+            concat_axis=0,
+        ),
+        ndim_at,
+    )
+    return tmp
+
+
+slots_close = functools.partial(assign_terms, comm_axis="tensor", ndim_at=0)
 
 
 def own_rows(so_far, axes):
@@ -104,7 +121,7 @@
     state = lax.dynamic_slice_in_dim(flat, start, count, 0).astype(jnp.float32) + mine
     square = of_everyone(jnp.sum(state * state, axis=1), PROMPT)
     owned = (state * lax.rsqrt(square / D + 1e-05)[:, None] * norm_gain).astype(jnp.bfloat16)
-    normed = lax.all_gather(owned, "tensor", axis=0, tiled=True)
+    normed = slots_close(owned)
     blocks = normed.reshape(variants, rows, share)
     mixed = jnp.tensordot(guidance, blocks.astype(jnp.float32), axes=1)
     high = mixed.astype(jnp.bfloat16)

time: 548 us -> 523 us (0.954)
  waiting for transfers between devices: 322 us -> 239 us
  blocking collectives: 106 us -> 169 us
    all_gather x1 -> x0, waiting for transfers between devices: 83.2 us -> none  [local(): normed = lax.all_gather(owned, 'tensor', axis=0, tiled=True)]
    all_to_all x0 -> x1, blocking collectives: none -> 64.3 us  [assign_terms(): lax.all_to_all(jnp.stack(lax.axis_size(comm_axis) * [page]), axis_name=co...]
    unnamed x17 -> x21, local copies, waits for them, and re-layouts: 26.5 us -> 26.5 us
    unnamed x1 -> x2, other arithmetic: 46.5 us -> 46.5 us
  transfers between devices with their start and end apart: 4 -> 3, of which waited for: 4 -> 3; matrix products, arithmetic and copies ran while one was open for 0% -> 0% of each run, Pallas kernels for 0% -> 0%
where the time goes in v1:
time: 523 us; the launch traced here: 522 us
  waiting for transfers between devices  239 us (46%)
  blocking collectives  169 us (32%)
  other arithmetic  55 us (11%)
  local copies, waits for them, and re-layouts  31.6 us (6%)
  matrix products  14 us (3%)
  between operations  13.3 us (3%)
    reduce_scatter x1, waiting for transfers between devices, local(): lax.psum_scatter(partial_branch, 'tensor', scatter_dimension=0, tiled=True)  124 us
    reduce_scatter x2, waiting for transfers between devices, own_rows(): so_far = lax.psum_scatter(so_far, axis, scatter_dimension=0, tiled=True)  114 us
    all_to_all x1, blocking collectives, assign_terms(): lax.all_to_all(jnp.stack(lax.axis_size(comm_axis) * [page]), axis_name=co...  64.3 us
    all_to_all x3, blocking collectives, copy_for_each(): lax.all_to_all(jnp.broadcast_to(array[None], (peers, *array.shape)), axis...  52.8 us
    unnamed x2, other arithmetic  46.5 us
    all_to_all x1, blocking collectives, local(): lax.all_to_all(tokens, PROMPT, split_axis=2, concat_axis=0, tiled=True)  31.1 us
    unnamed x21, local copies, waits for them, and re-layouts  26.5 us
    all_to_all x1, blocking collectives, sent_and_summed(): lax.all_to_all(tiles, axis, split_axis=0, concat_axis=0, tiled=True)  20.8 us
  transfers between devices with their start and end apart: 3, of which 3 were waited for; matrix products, arithmetic and copies ran while one was open for 0% of the time, Pallas kernels for 0%

profile of v1, /device:TPU:1, one launch (start us, length us, event | category | flops | bytes accessed | tf_op | source)
XLA Modules:
  0.0 522.0 jit_solution(16478993088200832191)
XLA Ops:
  6.5 0.0 copy-start
  6.5 0.0 reduce-scatter.4.cloned.1.call-start
  6.5 9.6 %copy.23 = bf16[1,128,8192]{1,0,2:T(2,128)(2,1)} copy(bf16[1,128,8192]{2,1,0:T(8,128)(2,1)} %param.8) | data formatting | bytes 4194304 | tf_op args[0]
  16.2 0.5 broadcast.20
  16.7 46.5 %reduce.1 = bf16[8192,128]{1,0:T(8,128)(2,1)} reduce(bf16[8192,1,128]{2,1,0:T(2,128)(2,1)} %bitcast.47, bf16[]{:T(256)} %broadcast.20), dimensions={1}, to_apply=%bitcast.29.reduce_sub_computation | reduce | bytes 4194306
  63.2 5.8 %reshape.55 = bf16[8,2,65536]{2,1,0:T(2,128)(2,1)} reshape(bf16[8192,128]{1,0:T(8,128)(2,1)} %reduce.1) | data formatting | bytes 4194304
  69.0 31.1 %all_to_all.41 = bf16[8,2,65536]{2,1,0:T(2,128)(2,1)} all-to-all(bf16[8,2,65536]{2,1,0:T(2,128)(2,1)} %reshape.55), channel_id=1, replica_groups=mesh['prompt_0'=4,'prompt_1'=2,'tensor'=32] {'prompt_0','prompt_1'}, dimensions={0} | all-to-all | bytes 4194304 | tf_op jit(solution)/shard_map/all_to_all | solution.py:108
  100.1 6.8 %reshape.56 = bf16[8192,1,128]{2,1,0:T(2,128)(2,1)} reshape(bf16[8,2,65536]{2,1,0:T(2,128)(2,1)} %all_to_all.41) | data formatting | bytes 4194304
  106.8 3.8 copy.30
  110.6 4.0 copy.24
  114.6 0.0 copy-start.1
  114.6 0.0 copy-start.5
  114.6 4.5 fusion.15
  119.1 0.0 copy-done.1
  119.1 0.0 copy-done.5
  119.1 2.2 fusion.16
  121.3 3.7 pad_maximum_fusion
  125.0 0.0 reduce-scatter.4.cloned.1.call-update
  125.0 0.0 reduce-scatter.6.cloned.1.call-start
  125.0 78.3 %reduce-scatter.4.cloned.1.call-done = f32[256,1792]{0,1:T(8,128)} async-done(((f32[1024,1792]{0,1:T(8,128)}), f32[256,1792]{0,1:T(8,128)}) %reduce-scatter.4.cloned.1.call-update) | async-done | bytes 1835024 | tf_op jit(solution)/shard_map/reduce_scatter | solution.py:30
  203.3 0.0 reduce-scatter.6.cloned.1.call-update
  203.4 0.2 reduce-scatter.8.cloned.1.call-start
  203.6 36.1 %reduce-scatter.6.cloned.1.call-done = f32[128,1792]{0,1:T(8,128)} async-done(((f32[256,1792]{0,1:T(8,128)}), f32[128,1792]{0,1:T(8,128)}) %reduce-scatter.6.cloned.1.call-update) | async-done | bytes 917520 | tf_op jit(solution)/shard_map/reduce_scatter | solution.py:30
  239.7 1.3 fusion.7
  240.9 0.2 copy.25
  241.1 0.2 broadcast_in_dim.6
  241.4 26.5 %all_to_all.42 = bf16[8,128,896]{2,1,0:T(8,128)(2,1)S(1)} all-to-all(bf16[8,128,896]{2,1,0:T(8,128)(2,1)S(1)} %broadcast_in_dim.6), channel_id=1, replica_groups=mesh['prompt_0'=4,'prompt_1'=2,'tensor'=32] {'prompt_0','prompt_1'}, dimensions={0} | all-to-all | bytes 3670016 | tf_op jit(solution)/shard_map/all_to_all | solution.py:36
  267.9 0.0 copy-done
  267.9 4.3 fusion.17
  272.2 0.0 copy-start.3
  272.2 0.0 slice-start
  272.2 0.0 reduce-scatter.8.cloned.1.call-update
  272.2 124.4 %reduce-scatter.8.cloned.1.call-done = f32[32,1024]{1,0:T(8,128)} async-done(((f32[1024,1024]{1,0:T(8,128)}), f32[32,1024]{1,0:T(8,128)}) %reduce-scatter.8.cloned.1.call-update) | async-done | bytes 131088 | tf_op jit(solution)/shard_map/reduce_scatter | solution.py:118
  396.6 1.0 multiply_reduce_fusion
  397.7 9.7 %all_to_all.43 = f32[8,1,32]{2,1,0:T(1,128)S(1)} all-to-all(f32[8,1,32]{2,1,0:T(1,128)S(1)} %broadcast_in_dim.7), channel_id=1, replica_groups=mesh['prompt_0'=4,'prompt_1'=2,'tensor'=32] {'prompt_0','prompt_1'}, dimensions={0} | all-to-all | bytes 2048 | tf_op jit(solution)/shard_map/all_to_all | solution.py:36
  407.4 0.0 copy-done.3
  407.4 1.0 multiply_convert_fusion
  408.4 0.2 stack.2
  408.6 0.0 copy-start.4
  408.6 0.0 slice-start.1
  408.7 64.3 %all_to_all.44 = bf16[32,32,1024]{2,1,0:T(8,128)(2,1)S(1)} all-to-all(bf16[32,32,1024]{2,1,0:T(8,128)(2,1)S(1)} %stack.2), channel_id=1, replica_groups=mesh['prompt_0'=4,'prompt_1'=2,'tensor'=32] {'tensor'}, dimensions={0} | all-to-all | bytes 4194304 | tf_op jit(solution)/shard_map/all_to_all | solution.py:14
  472.9 0.0 copy-done.4
  472.9 1.4 fusion
  474.3 0.1 copy.38
  474.4 0.1 fusion.6
  474.5 0.0 slice-done
  474.5 0.0 slice-done.1
  474.5 1.7 fusion.2
  476.2 0.1 slice_add_fusion
  476.4 0.0 copy-start.2
  476.4 20.8 %all_to_all.45 = f32[8,16,2688]{2,1,0:T(8,128)S(1)} all-to-all(f32[8,16,2688]{2,1,0:T(8,128)S(1)} %bitcast.51), channel_id=1, replica_groups=mesh['prompt_0'=4,'prompt_1'=2,'tensor'=32] {'prompt_0','prompt_1'}, dimensions={0} | all-to-all | bytes 2752512 | tf_op jit(solution)/shard_map/all_to_all | solution.py:64
  497.2 0.1 reduce_sum.38
  497.3 0.0 copy-done.2
  497.3 0.1 fusion.11
  497.5 0.2 exponential_reduce_fusion
  497.7 16.6 %all_to_all.46 = f32[32,2,16]{2,1,0:T(2,128)S(1)} all-to-all(f32[32,2,16]{2,1,0:T(2,128)S(1)} %broadcast_in_dim.8), channel_id=1, replica_groups=mesh['prompt_0'=4,'prompt_1'=2,'tensor'=32] {'tensor'}, dimensions={0} | all-to-all | bytes 8192 | tf_op jit(solution)/shard_map/all_to_all | solution.py:36
  514.7 0.8 subtract_subtract_fusion
  (28 shorter events, 0.5 us)
Async XLA Ops:
  6.5 261.4 %copy-start = (bf16[896,1024]{1,0:T(8,128)(2,1)S(1)}, bf16[896,1024]{1,0:T(8,128)(2,1)}, u32[]{:S(2)}) copy-start(bf16[896,1024]{1,0:T(8,128)(2,1)} %param.11) | copy-start | bytes 5505028
  6.5 196.8 %reduce-scatter.4.cloned.1.call-start = ((), (), s32[]{:S(2)}) async-start(), calls=%async_computation.9 | async-start | bytes 9175040 | tf_op jit(solution)/shard_map/reduce_scatter | solution.py:30
  114.6 4.5 copy-start.1
  114.6 4.5 copy-start.5
  125.0 114.7 %reduce-scatter.6.cloned.1.call-start = ((), (), s32[]{:S(2)}) async-start(), calls=%async_computation.10 | async-start | bytes 2752512 | tf_op jit(solution)/shard_map/reduce_scatter | solution.py:30
  203.4 193.3 %reduce-scatter.8.cloned.1.call-start = ((), (), s32[]{:S(2)}) async-start(), calls=%async_computation.11 | async-start | bytes 4325376 | tf_op jit(solution)/shard_map/reduce_scatter | solution.py:118
  272.2 135.2 %copy-start.3 = (f32[1024]{0:T(1024)S(1)}, f32[1024]{0:T(1024)}, u32[]{:S(2)}) copy-start(f32[1024]{0:T(1024)} %param.12) | copy-start | bytes 12292
  272.2 202.3 %slice-start = ((s8[5505024]{0:T(1024)(128)(4,1)}), s8[1310720]{0:T(1024)(128)(4,1)S(1)}, s32[]{:S(2)}) async-start(s8[5505024]{0:T(1024)(128)(4,1)} %bitcast.65), calls=%async_computation.12 | async-start | bytes 2621440
  408.6 64.3 %copy-start.4 = (f32[8]{0:T(128)S(1)}, f32[8]{0:T(128)}, u32[]{:S(2)}) copy-start(f32[8]{0:T(128)} %param.14) | copy-start | bytes 100
  408.6 65.9 %slice-start.1 = ((s8[5505024]{0:T(1024)(128)(4,1)}), s8[4194304]{0:T(1024)(128)(4,1)S(1)}, s32[]{:S(2)}) async-start(s8[5505024]{0:T(1024)(128)(4,1)} %bitcast.65), calls=%async_computation.13 | async-start | bytes 8388608
  476.4 20.9 %copy-start.2 = (f32[16,2688]{1,0:T(8,128)S(1)}, f32[16,2688]{1,0:T(8,128)}, u32[]{:S(2)}) copy-start(f32[16,2688]{1,0:T(8,128)} %param.15) | copy-start | bytes 516100
Sparse Core Ops, SparseCore 0:
  125.1 78.1 reduce-scatter.3
  205.8 33.7 reduce-scatter.5
  272.3 124.2 reduce-scatter.7
